TPU v7x, 32 devices: a whole 2x2x4 slice. The times are simulated.
32 devices in a mesh: prow: 16 (over z, x, core), pcol: 2 (over y).
Axes of the slice: x: 2, y: 2, z: 4, core: 2. Of those that a mesh axis runs over, the one named last changes fastest.
Arguments:
- panel: bfloat16 [8192, 4096], P('prow', 'pcol'), may hold values from -0.09375 to 0.09375
- anc_inverse: bfloat16 [8192, 8192], P('prow', 'pcol'), may hold values from -6 to 6
- diag_inverse: bfloat16 [4096, 4096], P('prow', 'pcol'), may hold values from -6 to 6
- block_counts: int32 [16], replicated, may hold values from 0 to 4, as said below
Outputs:
- off_diag: bfloat16 [8192, 4096], P('prow', 'pcol')
- diag_block: float32 [4096, 4096], P('prow', 'pcol')
Inputs may be any that keep to these rules, and one draw needn't show every extreme that they name: `block_counts`: they add up to exactly 32, and some grid row owns 4 blocks.
All inputs are finite; a program needn't handle non-finite values.
Results may differ from a plain program's by a relative error of at most 0.002.
Values may be sent and summed in bfloat16 or wider, within the bound.
No kernel may reach another device: no remote copies, remote signals or barrier semaphores. Data moves between devices by JAX's collectives and lax.ppermute only.
A program may use at most 128 MiB of HBM per device.

v0:
```python
import jax
import jax.numpy as jnp
from jax import lax
from jax.sharding import PartitionSpec as P

BLK = 128


def per_device(panel, anc_inverse, diag_inverse, block_counts):
    grid_row = lax.axis_index("prow")
    slot_rows = panel.shape[0]
    own_count = block_counts[grid_row]
    in_use = jnp.arange(slot_rows) // BLK < own_count
    masked = jnp.where(in_use[:, None], panel, jnp.zeros_like(panel))
    whole_rows = lax.all_gather(masked, "pcol", axis=1, tiled=True)
    all_panel = lax.all_gather(masked, "prow", axis=0, tiled=True)
    all_inverse = lax.all_gather(anc_inverse, "pcol", axis=1, tiled=True)
    product = jnp.dot(all_inverse, all_panel, preferred_element_type=jnp.float32)
    off_diag = jnp.where(in_use[:, None], -product, 0.0).astype(jnp.bfloat16)
    summed = lax.psum_scatter(
        lax.dot_general(
            whole_rows, off_diag, (((0,), (0,)), ((), ())), preferred_element_type=jnp.float32
        ),
        "prow",
        scatter_dimension=0,
        tiled=True,
    )
    diag_block = diag_inverse.astype(jnp.float32) - summed
    return (off_diag, diag_block)


def solution(mesh):
    return jax.shard_map(
        per_device,
        mesh=mesh,
        in_specs=(P("prow", "pcol"), P("prow", "pcol"), P("prow", "pcol"), P()),
        out_specs=(P("prow", "pcol"), P("prow", "pcol")),
        check_vma=False,
    )
```

profile of v0, /device:TPU:0, one launch (start us, length us, event | category | flops | bytes accessed | tf_op | source)
XLA Modules:
  0.0 703.6 jit_solution(9929988382303146813)
XLA Ops:
  7.2 0.0 copy-start.2
  7.2 0.0 copy-start
  7.2 0.0 all-gather.6.cloned.1.call-start
  7.2 0.7 all-gather.6.cloned.1.call-update
  7.9 0.0 all-gather.4.cloned.1.call-start
  8.0 0.0 copy-done.2
  8.0 0.6 dynamic_slice.3
  8.6 0.7 fusion
  9.2 0.0 copy-done
  9.2 1.5 broadcast_select_fusion
  10.8 0.0 all-gather.4.cloned.1.call-update
  10.8 0.0 all-gather.8.cloned.1.call-start
  10.8 0.7 all-gather.8.cloned.1.call-update
  11.5 0.0 reduce-scatter.2.cloned.1.call-start
  11.6 104.7 %all-gather.6.cloned.1.call-done = bf16[512,8192]{1,0:T(8,128)(2,1)} async-done(((bf16[512,4096]{1,0:T(8,128)(2,1)}), bf16[512,8192]{1,0:T(8,128)(2,1)}) %all-gather.6.cloned.1.call-update) | async-done | bytes 8388624 | tf_op jit(solution)/shard_map/all_gather | solution.py:17
  116.3 170.2 %all-gather.4.cloned.1.call-done = bf16[8192,2048]{1,0:T(8,128)(2,1)} async-done(((bf16[512,2048]{1,0:T(8,128)(2,1)}), bf16[8192,2048]{1,0:T(8,128)(2,1)}) %all-gather.4.cloned.1.call-update) | async-done | bytes 33554448 | tf_op jit(solution)/shard_map/all_gather | solution.py:16
  286.5 24.0 %select_convert_fusion = bf16[2048,512]{1,0:T(8,128)(2,1)S(1)} fusion(bf16[8192,2048]{1,0:T(8,128)(2,1)} %all-gather.4.cloned.1.call-done, bf16[512,8192]{1,0:T(8,128)(2,1)} %all-gather.6.cloned.1.call-done, pred[512]{0:T(512)(128)(4,1)S(1)} %fusion), kind=kOutput, calls=%fused_computation | convolution fusion | flops 17183014912 | bytes 44040704 | tf_op jit(solution)/shard_map/dot_general | solution.py:18
  310.5 34.8 %all-gather.8.cloned.1.call-done = bf16[512,4096]{1,0:T(8,128)(2,1)} async-done(((bf16[512,2048]{1,0:T(8,128)(2,1)}), bf16[512,4096]{1,0:T(8,128)(2,1)}) %all-gather.8.cloned.1.call-update) | async-done | bytes 4194320 | tf_op jit(solution)/shard_map/all_gather | solution.py:15
  345.4 17.6 %fusion.4 = f32[4096,2048]{1,0:T(8,128)} fusion(bf16[512,4096]{1,0:T(8,128)(2,1)} %all-gather.8.cloned.1.call-done, bf16[2048,512]{1,0:T(8,128)(2,1)S(1)} %select_convert_fusion), kind=kOutput, calls=%fused_computation.11 | convolution fusion | flops 8589934592 | bytes 39845888 | tf_op jit(solution)/shard_map/dot_general | solution.py:21
  363.0 0.0 reduce-scatter.2.cloned.1.call-update
  363.0 0.0 copy-start.1
  363.0 2.4 copy.6
  365.4 328.4 %reduce-scatter.2.cloned.1.call-done = f32[256,2048]{1,0:T(8,128)} async-done(((f32[4096,2048]{1,0:T(8,128)}), f32[256,2048]{1,0:T(8,128)}) %reduce-scatter.2.cloned.1.call-update) | async-done | bytes 2097168 | tf_op jit(solution)/shard_map/reduce_scatter | solution.py:20
  693.8 0.0 copy-done.1
  693.8 3.3 convert_subtract_fusion
Async XLA Ops:
  7.2 0.8 copy-start.2
  7.2 2.1 copy-start
  7.2 109.1 %all-gather.6.cloned.1.call-start = ((), (), s32[]{:S(2)}) async-start(), calls=%async_computation.2 | async-start | bytes 12582912 | tf_op jit(solution)/shard_map/all_gather | solution.py:17
  7.9 278.6 %all-gather.4.cloned.1.call-start = ((), (), s32[]{:S(2)}) async-start(), calls=%async_computation.1 | async-start | bytes 35651584 | tf_op jit(solution)/shard_map/all_gather | solution.py:16
  10.8 334.6 %all-gather.8.cloned.1.call-start = ((), (), s32[]{:S(2)}) async-start(), calls=%async_computation.3 | async-start | bytes 6291456 | tf_op jit(solution)/shard_map/all_gather | solution.py:15
  11.5 682.3 %reduce-scatter.2.cloned.1.call-start = ((), (), s32[]{:S(2)}) async-start(), calls=%async_computation.4 | async-start | bytes 35651584 | tf_op jit(solution)/shard_map/reduce_scatter | solution.py:20
  363.0 330.8 %copy-start.1 = (bf16[256,2048]{1,0:T(8,128)(2,1)S(1)}, bf16[256,2048]{1,0:T(8,128)(2,1)}, u32[]{:S(2)}) copy-start(bf16[256,2048]{1,0:T(8,128)(2,1)} %param.6) | copy-start | bytes 3145732
Sparse Core Ops, SparseCore 0:
  9.5 106.6 all-gather.5
  118.4 168.0 all-gather.3
  288.6 56.6 all-gather.7
  363.2 330.5 reduce-scatter.1
where the time goes:
time: 704 us
  waiting for transfers between devices  640 us (91%)
  matrix products  41.6 us (6%)
  between operations  13.8 us (2%)
    reduce_scatter x1, waiting for transfers between devices, per_device(): lax.psum_scatter(lax.dot_general(whole_rows, off_diag, (((0,), (0,)), (()...  328 us
    all_gather x1, waiting for transfers between devices, per_device(): all_panel = lax.all_gather(masked, 'prow', axis=0, tiled=True)  170 us
    all_gather x1, waiting for transfers between devices, per_device(): all_inverse = lax.all_gather(anc_inverse, 'pcol', axis=1, tiled=True)  105 us
    all_gather x1, waiting for transfers between devices, per_device(): whole_rows = lax.all_gather(masked, 'pcol', axis=1, tiled=True)  34.8 us
    dot_general x1, matrix products, per_device(): jnp.dot(all_inverse, all_panel, preferred_element_type=jnp.float32)  24 us
    dot_general x1, matrix products, per_device(): lax.dot_general(whole_rows, off_diag, (((0,), (0,)), ((), ())), preferred...  17.6 us
  transfers between devices with their start and end apart: 4, of which 4 were waited for; matrix products, arithmetic and copies ran while one was open for 4% of the time, Pallas kernels for 0%

commit v1 on v0

--- a/solution.py
+++ b/solution.py
@@ -2,6 +2,7 @@
 import jax.numpy as jnp
 from jax import lax
 from jax.sharding import PartitionSpec as P
+from jax.lax import axis_index, ppermute, psum
 
 BLK = 128
 
@@ -13,7 +14,15 @@
     in_use = jnp.arange(slot_rows) // BLK < own_count
     masked = jnp.where(in_use[:, None], panel, jnp.zeros_like(panel))
     whole_rows = lax.all_gather(masked, "pcol", axis=1, tiled=True)
-    all_panel = lax.all_gather(masked, "prow", axis=0, tiled=True)
+    shares = psum(1, "prow")
+    aux = [None] * shares
+    series = [(it, (it + 1) % shares) for it in range(shares)]
+    aux[shares - 1] = masked
+    for ix in range(shares - 2, -1, -1):
+        aux[ix] = ppermute(aux[ix + 1], "prow", series)
+    x_new = jnp.concatenate(aux, axis=0)
+    fresh = (axis_index("prow") + 1) * masked.shape[0]
+    all_panel = jnp.roll(x_new, fresh, axis=0)
     all_inverse = lax.all_gather(anc_inverse, "pcol", axis=1, tiled=True)
     product = jnp.dot(all_inverse, all_panel, preferred_element_type=jnp.float32)
     off_diag = jnp.where(in_use[:, None], -product, 0.0).astype(jnp.bfloat16)

time: 704 us -> 913 us (1.30)
  waiting for transfers between devices: 640 us -> 750 us
  local copies, waits for them, and re-layouts: 2.98 us -> 95.6 us
    ppermute x0 -> x15, waiting for transfers between devices: none -> 424 us  [per_device(): aux[ix] = ppermute(aux[ix + 1], 'prow', series)]
    all_gather x1 -> x0, waiting for transfers between devices: 170 us -> none  [per_device(): all_panel = lax.all_gather(masked, 'prow', axis=0, tiled=True)]
    all_gather x1, waiting for transfers between devices: 105 us -> 0.01 us  [per_device(): all_inverse = lax.all_gather(anc_inverse, 'pcol', axis=1, tiled=True)]
    unnamed x7 -> x79, local copies, waits for them, and re-layouts: 2.39 us -> 94.2 us
    all_gather x1, waiting for transfers between devices: 34.8 us -> 0.02 us  [per_device(): whole_rows = lax.all_gather(masked, 'pcol', axis=1, tiled=True)]
  transfers between devices with their start and end apart: 4 -> 18, of which waited for: 4 -> 16; matrix products, arithmetic and copies ran while one was open for 4% -> 12% of each run, Pallas kernels for 0% -> 0%
where the time goes in v1:
time: 913 us; the launch traced here: 912 us
  waiting for transfers between devices  750 us (82%)
  local copies, waits for them, and re-layouts  95.6 us (10%)
  matrix products  41.6 us (5%)
  between operations  13.9 us (2%)
  other arithmetic  10.5 us (1%)
    ppermute x15, waiting for transfers between devices, per_device(): aux[ix] = ppermute(aux[ix + 1], 'prow', series)  424 us
    reduce_scatter x1, waiting for transfers between devices, per_device(): lax.psum_scatter(lax.dot_general(whole_rows, off_diag, (((0,), (0,)), (()...  326 us
    unnamed x79, local copies, waits for them, and re-layouts  94.2 us
    dot_general x1, matrix products, per_device(): jnp.dot(all_inverse, all_panel, preferred_element_type=jnp.float32)  24 us
  transfers between devices with their start and end apart: 18, of which 16 were waited for; matrix products, arithmetic and copies ran while one was open for 12% of the time, Pallas kernels for 0%

profile of v1, /device:TPU:0, one launch (start us, length us, event | category | flops | bytes accessed | tf_op | source)
XLA Modules:
  0.0 912.3 jit_solution(17857974493092935983)
XLA Ops:
  7.2 1.4 dynamic_slice.7
  9.3 3.1 broadcast_select_fusion
  12.9 28.9 %collective-permute-done = bf16[512,2048]{1,0:T(8,128)(2,1)S(1)} collective-permute-done((bf16[512,2048]{1,0:T(8,128)(2,1)}, bf16[512,2048]{1,0:T(8,128)(2,1)S(1)}, u32[]{:S(2)}, u32[]{:S(2)}) %collective-permute-start) | collective-permute-done | bytes 2097184 | tf_op jit(solution)/shard_map/ppermute | solution.py:22
  41.8 1.3 copy-done.1
  43.1 28.2 %collective-permute-done.1 = bf16[512,2048]{1,0:T(8,128)(2,1)S(1)} collective-permute-done((bf16[512,2048]{1,0:T(8,128)(2,1)S(1)}, bf16[512,2048]{1,0:T(8,128)(2,1)S(1)}, u32[]{:S(2)}, u32[]{:S(2)}) %collective-permute-start.1) | collective-permute-done | bytes 2097184 | tf_op jit(solution)/shard_map/ppermute | solution.py:22
  71.2 1.3 copy-done.3
  72.6 28.2 %collective-permute-done.2 = bf16[512,2048]{1,0:T(8,128)(2,1)S(1)} collective-permute-done((bf16[512,2048]{1,0:T(8,128)(2,1)S(1)}, bf16[512,2048]{1,0:T(8,128)(2,1)S(1)}, u32[]{:S(2)}, u32[]{:S(2)}) %collective-permute-start.2) | collective-permute-done | bytes 2097184 | tf_op jit(solution)/shard_map/ppermute | solution.py:22
  100.7 1.4 copy-done.5
  102.1 28.2 %collective-permute-done.3 = bf16[512,2048]{1,0:T(8,128)(2,1)S(1)} collective-permute-done((bf16[512,2048]{1,0:T(8,128)(2,1)S(1)}, bf16[512,2048]{1,0:T(8,128)(2,1)S(1)}, u32[]{:S(2)}, u32[]{:S(2)}) %collective-permute-start.3) | collective-permute-done | bytes 2097184 | tf_op jit(solution)/shard_map/ppermute | solution.py:22
  130.3 1.4 copy-done.7
  131.6 28.2 %collective-permute-done.4 = bf16[512,2048]{1,0:T(8,128)(2,1)S(1)} collective-permute-done((bf16[512,2048]{1,0:T(8,128)(2,1)S(1)}, bf16[512,2048]{1,0:T(8,128)(2,1)S(1)}, u32[]{:S(2)}, u32[]{:S(2)}) %collective-permute-start.4) | collective-permute-done | bytes 2097184 | tf_op jit(solution)/shard_map/ppermute | solution.py:22
  159.8 1.3 copy-done.9
  161.1 28.2 %collective-permute-done.5 = bf16[512,2048]{1,0:T(8,128)(2,1)S(1)} collective-permute-done((bf16[512,2048]{1,0:T(8,128)(2,1)S(1)}, bf16[512,2048]{1,0:T(8,128)(2,1)S(1)}, u32[]{:S(2)}, u32[]{:S(2)}) %collective-permute-start.5) | collective-permute-done | bytes 2097184 | tf_op jit(solution)/shard_map/ppermute | solution.py:22
  189.3 1.3 copy-done.11
  190.6 28.2 %collective-permute-done.6 = bf16[512,2048]{1,0:T(8,128)(2,1)S(1)} collective-permute-done((bf16[512,2048]{1,0:T(8,128)(2,1)S(1)}, bf16[512,2048]{1,0:T(8,128)(2,1)S(1)}, u32[]{:S(2)}, u32[]{:S(2)}) %collective-permute-start.6) | collective-permute-done | bytes 2097184 | tf_op jit(solution)/shard_map/ppermute | solution.py:22
  220.1 28.2 %collective-permute-done.7 = bf16[512,2048]{1,0:T(8,128)(2,1)S(1)} collective-permute-done((bf16[512,2048]{1,0:T(8,128)(2,1)S(1)}, bf16[512,2048]{1,0:T(8,128)(2,1)S(1)}, u32[]{:S(2)}, u32[]{:S(2)}) %collective-permute-start.7) | collective-permute-done | bytes 2097184 | tf_op jit(solution)/shard_map/ppermute | solution.py:22
  248.2 1.4 copy-done.15
  249.7 28.2 %collective-permute-done.8 = bf16[512,2048]{1,0:T(8,128)(2,1)S(1)} collective-permute-done((bf16[512,2048]{1,0:T(8,128)(2,1)S(1)}, bf16[512,2048]{1,0:T(8,128)(2,1)S(1)}, u32[]{:S(2)}, u32[]{:S(2)}) %collective-permute-start.8) | collective-permute-done | bytes 2097184 | tf_op jit(solution)/shard_map/ppermute | solution.py:22
  277.8 1.3 copy-done.17
  279.2 28.3 %collective-permute-done.9 = bf16[512,2048]{1,0:T(8,128)(2,1)} collective-permute-done((bf16[512,2048]{1,0:T(8,128)(2,1)S(1)}, bf16[512,2048]{1,0:T(8,128)(2,1)}, u32[]{:S(2)}, u32[]{:S(2)}) %collective-permute-start.9) | collective-permute-done | bytes 2097184 | tf_op jit(solution)/shard_map/ppermute | solution.py:22
  307.5 28.4 %collective-permute-done.10 = bf16[512,2048]{1,0:T(8,128)(2,1)} collective-permute-done((bf16[512,2048]{1,0:T(8,128)(2,1)}, bf16[512,2048]{1,0:T(8,128)(2,1)}, u32[]{:S(2)}, u32[]{:S(2)}) %collective-permute-start.10) | collective-permute-done | bytes 2097184 | tf_op jit(solution)/shard_map/ppermute | solution.py:22
  335.9 28.4 %collective-permute-done.11 = bf16[512,2048]{1,0:T(8,128)(2,1)S(1)} collective-permute-done((bf16[512,2048]{1,0:T(8,128)(2,1)}, bf16[512,2048]{1,0:T(8,128)(2,1)S(1)}, u32[]{:S(2)}, u32[]{:S(2)}) %collective-permute-start.11) | collective-permute-done | bytes 2097184 | tf_op jit(solution)/shard_map/ppermute | solution.py:22
  364.3 1.3 copy-done.19
  365.6 28.2 %collective-permute-done.12 = bf16[512,2048]{1,0:T(8,128)(2,1)S(1)} collective-permute-done((bf16[512,2048]{1,0:T(8,128)(2,1)S(1)}, bf16[512,2048]{1,0:T(8,128)(2,1)S(1)}, u32[]{:S(2)}, u32[]{:S(2)}) %collective-permute-start.12) | collective-permute-done | bytes 2097184 | tf_op jit(solution)/shard_map/ppermute | solution.py:22
  393.7 1.3 copy-done.21
  395.1 28.3 %collective-permute-done.13 = bf16[512,2048]{1,0:T(8,128)(2,1)} collective-permute-done((bf16[512,2048]{1,0:T(8,128)(2,1)S(1)}, bf16[512,2048]{1,0:T(8,128)(2,1)}, u32[]{:S(2)}, u32[]{:S(2)}) %collective-permute-start.13) | collective-permute-done | bytes 2097184 | tf_op jit(solution)/shard_map/ppermute | solution.py:22
  423.5 28.3 %collective-permute-done.14 = bf16[512,2048]{1,0:T(8,128)(2,1)} collective-permute-done((bf16[512,2048]{1,0:T(8,128)(2,1)}, bf16[512,2048]{1,0:T(8,128)(2,1)}, u32[]{:S(2)}, u32[]{:S(2)}) %collective-permute-start.14) | collective-permute-done | bytes 2097184 | tf_op jit(solution)/shard_map/ppermute | solution.py:22
  451.8 3.2 constant_dynamic-update-slice_fusion.31
  455.0 3.2 constant_dynamic-update-slice_fusion.30
  458.2 3.2 constant_dynamic-update-slice_fusion.29
  461.4 3.2 constant_dynamic-update-slice_fusion.28
  464.6 3.2 constant_dynamic-update-slice_fusion.27
  467.8 3.2 constant_dynamic-update-slice_fusion.26
  471.0 3.1 constant_dynamic-update-slice_fusion.25
  474.1 3.1 constant_dynamic-update-slice_fusion.24
  477.3 3.2 constant_dynamic-update-slice_fusion.23
  480.5 3.2 constant_dynamic-update-slice_fusion.22
  483.6 3.2 constant_dynamic-update-slice_fusion.21
  486.8 3.2 constant_dynamic-update-slice_fusion.20
  490.1 3.2 constant_dynamic-update-slice_fusion.19
  493.3 3.2 constant_dynamic-update-slice_fusion.18
  496.5 3.1 constant_dynamic-update-slice_fusion.17
  499.6 1.7 constant_dynamic-update-slice_fusion.16
  501.4 3.2 constant_dynamic-update-slice_fusion.15
  504.6 3.2 constant_dynamic-update-slice_fusion.14
  507.7 1.5 constant_dynamic-update-slice_fusion.13
  509.2 1.5 constant_dynamic-update-slice_fusion.12
  510.7 3.2 constant_dynamic-update-slice_fusion.11
  513.9 3.2 constant_dynamic-update-slice_fusion.10
  517.1 1.5 constant_dynamic-update-slice_fusion.9
  518.6 1.5 constant_dynamic-update-slice_fusion.8
  520.1 1.5 constant_dynamic-update-slice_fusion.7
  521.6 1.5 constant_dynamic-update-slice_fusion.6
  523.1 1.5 constant_dynamic-update-slice_fusion.5
  524.6 1.5 constant_dynamic-update-slice_fusion.4
  526.1 1.5 constant_dynamic-update-slice_fusion.3
  527.6 1.5 constant_dynamic-update-slice_fusion.2
  529.1 1.5 constant_dynamic-update-slice_fusion.1
  530.6 1.7 constant_dynamic-update-slice_fusion
  532.3 24.0 %select_convert_fusion = bf16[2048,512]{1,0:T(8,128)(2,1)S(1)} fusion(bf16[512,8192]{1,0:T(8,128)(2,1)} %all-gather.3.cloned.1.call-done, bf16[16384,2048]{1,0:T(8,128)(2,1)} %constant_dynamic-update-slice_fusion, s32[]{:T(128)S(6)} %select_n.38, pred[512]{0:T(512)(128)(4,1)S(1)} %fusion.4), kind=kOutput, calls=%fused_computation.2 | convolution fusion | flops 17183014912 | bytes 44040708 | tf_op jit(solution)/shard_map/dot_general | solution.py:27
  556.4 17.6 %fusion.9 = f32[4096,2048]{1,0:T(8,128)} fusion(bf16[512,4096]{1,0:T(8,128)(2,1)} %all-gather.5.cloned.1.call-done, bf16[2048,512]{1,0:T(8,128)(2,1)S(1)} %select_convert_fusion), kind=kOutput, calls=%fused_computation.46 | convolution fusion | flops 8589934592 | bytes 39845888 | tf_op jit(solution)/shard_map/dot_general | solution.py:30
  574.0 2.4 copy.6
  576.4 326.1 %reduce-scatter.2.cloned.1.call-done = f32[256,2048]{1,0:T(8,128)} async-done(((f32[4096,2048]{1,0:T(8,128)}), f32[256,2048]{1,0:T(8,128)}) %reduce-scatter.2.cloned.1.call-update) | async-done | bytes 2097168 | tf_op jit(solution)/shard_map/reduce_scatter | solution.py:29
  902.5 3.3 convert_subtract_fusion
  (62 shorter events, 2.7 us)
Async XLA Ops:
  7.2 492.5 %copy-start = (bf16[512,2048]{1,0:T(8,128)(2,1)S(1)}, bf16[512,2048]{1,0:T(8,128)(2,1)}, u32[]{:S(2)}) copy-start(bf16[512,2048]{1,0:T(8,128)(2,1)} %param.4) | copy-start | bytes 6291460
  7.2 525.2 %all-gather.3.cloned.1.call-start = ((), (), s32[]{:S(2)}) async-start(), calls=%async_computation.1 | async-start | bytes 12582912 | tf_op jit(solution)/shard_map/all_gather | solution.py:26
  12.4 29.4 %collective-permute-start = (bf16[512,2048]{1,0:T(8,128)(2,1)}, bf16[512,2048]{1,0:T(8,128)(2,1)S(1)}, u32[]{:S(2)}, u32[]{:S(2)}) collective-permute-start(bf16[512,2048]{1,0:T(8,128)(2,1)} %broadcast_select_fusion), channel_id=1, source_target_pairs={{0,2},{2,4},{4,6},{6,8},{8,10},{10,12},{12,14},{14,16},{16,18},{18... | collective-permute-start | bytes 6291464 | tf_op jit(solution)/shard_map/ppermute | solution.py:22
  41.8 1.3 copy-start.1
  43.1 28.2 %collective-permute-start.1 = (bf16[512,2048]{1,0:T(8,128)(2,1)S(1)}, bf16[512,2048]{1,0:T(8,128)(2,1)S(1)}, u32[]{:S(2)}, u32[]{:S(2)}) collective-permute-start(bf16[512,2048]{1,0:T(8,128)(2,1)S(1)} %collective-permute-done), channel_id=1, source_target_pairs={{0,2},{2,4},{4,6},{6,8},{8,10},{10,12},{12,14},{14,16},{16,18},{18... | collective-permute-start | bytes 6291464 | tf_op jit(solution)/shard_map/ppermute | solution.py:22
  71.2 1.3 copy-start.3
  72.6 28.2 %collective-permute-start.2 = (bf16[512,2048]{1,0:T(8,128)(2,1)S(1)}, bf16[512,2048]{1,0:T(8,128)(2,1)S(1)}, u32[]{:S(2)}, u32[]{:S(2)}) collective-permute-start(bf16[512,2048]{1,0:T(8,128)(2,1)S(1)} %collective-permute-done.1), channel_id=1, source_target_pairs={{0,2},{2,4},{4,6},{6,8},{8,10},{10,12},{12,14},{14,16},{16,18},{18... | collective-permute-start | bytes 6291464 | tf_op jit(solution)/shard_map/ppermute | solution.py:22
  100.7 1.4 copy-start.5
  102.1 28.2 %collective-permute-start.3 = (bf16[512,2048]{1,0:T(8,128)(2,1)S(1)}, bf16[512,2048]{1,0:T(8,128)(2,1)S(1)}, u32[]{:S(2)}, u32[]{:S(2)}) collective-permute-start(bf16[512,2048]{1,0:T(8,128)(2,1)S(1)} %collective-permute-done.2), channel_id=1, source_target_pairs={{0,2},{2,4},{4,6},{6,8},{8,10},{10,12},{12,14},{14,16},{16,18},{18... | collective-permute-start | bytes 6291464 | tf_op jit(solution)/shard_map/ppermute | solution.py:22
  130.3 1.4 copy-start.7
  131.6 28.2 %collective-permute-start.4 = (bf16[512,2048]{1,0:T(8,128)(2,1)S(1)}, bf16[512,2048]{1,0:T(8,128)(2,1)S(1)}, u32[]{:S(2)}, u32[]{:S(2)}) collective-permute-start(bf16[512,2048]{1,0:T(8,128)(2,1)S(1)} %collective-permute-done.3), channel_id=1, source_target_pairs={{0,2},{2,4},{4,6},{6,8},{8,10},{10,12},{12,14},{14,16},{16,18},{18... | collective-permute-start | bytes 6291464 | tf_op jit(solution)/shard_map/ppermute | solution.py:22
  159.8 1.3 copy-start.9
  161.1 28.2 %collective-permute-start.5 = (bf16[512,2048]{1,0:T(8,128)(2,1)S(1)}, bf16[512,2048]{1,0:T(8,128)(2,1)S(1)}, u32[]{:S(2)}, u32[]{:S(2)}) collective-permute-start(bf16[512,2048]{1,0:T(8,128)(2,1)S(1)} %collective-permute-done.4), channel_id=1, source_target_pairs={{0,2},{2,4},{4,6},{6,8},{8,10},{10,12},{12,14},{14,16},{16,18},{18... | collective-permute-start | bytes 6291464 | tf_op jit(solution)/shard_map/ppermute | solution.py:22
  189.3 1.3 copy-start.11
  190.6 28.2 %collective-permute-start.6 = (bf16[512,2048]{1,0:T(8,128)(2,1)S(1)}, bf16[512,2048]{1,0:T(8,128)(2,1)S(1)}, u32[]{:S(2)}, u32[]{:S(2)}) collective-permute-start(bf16[512,2048]{1,0:T(8,128)(2,1)S(1)} %collective-permute-done.5), channel_id=1, source_target_pairs={{0,2},{2,4},{4,6},{6,8},{8,10},{10,12},{12,14},{14,16},{16,18},{18... | collective-permute-start | bytes 6291464 | tf_op jit(solution)/shard_map/ppermute | solution.py:22
  218.8 1.3 copy-start.13
  220.1 28.2 %collective-permute-start.7 = (bf16[512,2048]{1,0:T(8,128)(2,1)S(1)}, bf16[512,2048]{1,0:T(8,128)(2,1)S(1)}, u32[]{:S(2)}, u32[]{:S(2)}) collective-permute-start(bf16[512,2048]{1,0:T(8,128)(2,1)S(1)} %collective-permute-done.6), channel_id=1, source_target_pairs={{0,2},{2,4},{4,6},{6,8},{8,10},{10,12},{12,14},{14,16},{16,18},{18... | collective-permute-start | bytes 6291464 | tf_op jit(solution)/shard_map/ppermute | solution.py:22
  248.2 1.4 copy-start.15
  249.7 28.2 %collective-permute-start.8 = (bf16[512,2048]{1,0:T(8,128)(2,1)S(1)}, bf16[512,2048]{1,0:T(8,128)(2,1)S(1)}, u32[]{:S(2)}, u32[]{:S(2)}) collective-permute-start(bf16[512,2048]{1,0:T(8,128)(2,1)S(1)} %collective-permute-done.7), channel_id=1, source_target_pairs={{0,2},{2,4},{4,6},{6,8},{8,10},{10,12},{12,14},{14,16},{16,18},{18... | collective-permute-start | bytes 6291464 | tf_op jit(solution)/shard_map/ppermute | solution.py:22
  277.8 1.3 copy-start.17
  279.2 28.3 %collective-permute-start.9 = (bf16[512,2048]{1,0:T(8,128)(2,1)S(1)}, bf16[512,2048]{1,0:T(8,128)(2,1)}, u32[]{:S(2)}, u32[]{:S(2)}) collective-permute-start(bf16[512,2048]{1,0:T(8,128)(2,1)S(1)} %collective-permute-done.8), channel_id=1, source_target_pairs={{0,2},{2,4},{4,6},{6,8},{8,10},{10,12},{12,14},{14,16},{16,18},{18... | collective-permute-start | bytes 6291464 | tf_op jit(solution)/shard_map/ppermute | solution.py:22
  307.4 28.5 %collective-permute-start.10 = (bf16[512,2048]{1,0:T(8,128)(2,1)}, bf16[512,2048]{1,0:T(8,128)(2,1)}, u32[]{:S(2)}, u32[]{:S(2)}) collective-permute-start(bf16[512,2048]{1,0:T(8,128)(2,1)} %collective-permute-done.9), channel_id=1, source_target_pairs={{0,2},{2,4},{4,6},{6,8},{8,10},{10,12},{12,14},{14,16},{16,18},{18... | collective-permute-start | bytes 6291464 | tf_op jit(solution)/shard_map/ppermute | solution.py:22
  307.4 248.9 %all-gather.5.cloned.1.call-start = ((), (), s32[]{:S(2)}) async-start(), calls=%async_computation.2 | async-start | bytes 6291456 | tf_op jit(solution)/shard_map/all_gather | solution.py:16
  335.9 28.4 %collective-permute-start.11 = (bf16[512,2048]{1,0:T(8,128)(2,1)}, bf16[512,2048]{1,0:T(8,128)(2,1)S(1)}, u32[]{:S(2)}, u32[]{:S(2)}) collective-permute-start(bf16[512,2048]{1,0:T(8,128)(2,1)} %collective-permute-done.10), channel_id=1, source_target_pairs={{0,2},{2,4},{4,6},{6,8},{8,10},{10,12},{12,14},{14,16},{16,18},{18... | collective-permute-start | bytes 6291464 | tf_op jit(solution)/shard_map/ppermute | solution.py:22
  364.3 1.3 copy-start.19
  365.6 28.2 %collective-permute-start.12 = (bf16[512,2048]{1,0:T(8,128)(2,1)S(1)}, bf16[512,2048]{1,0:T(8,128)(2,1)S(1)}, u32[]{:S(2)}, u32[]{:S(2)}) collective-permute-start(bf16[512,2048]{1,0:T(8,128)(2,1)S(1)} %collective-permute-done.11), channel_id=1, source_target_pairs={{0,2},{2,4},{4,6},{6,8},{8,10},{10,12},{12,14},{14,16},{16,18},{18... | collective-permute-start | bytes 6291464 | tf_op jit(solution)/shard_map/ppermute | solution.py:22
  393.7 1.3 copy-start.21
  395.1 28.3 %collective-permute-start.13 = (bf16[512,2048]{1,0:T(8,128)(2,1)S(1)}, bf16[512,2048]{1,0:T(8,128)(2,1)}, u32[]{:S(2)}, u32[]{:S(2)}) collective-permute-start(bf16[512,2048]{1,0:T(8,128)(2,1)S(1)} %collective-permute-done.12), channel_id=1, source_target_pairs={{0,2},{2,4},{4,6},{6,8},{8,10},{10,12},{12,14},{14,16},{16,18},{18... | collective-permute-start | bytes 6291464 | tf_op jit(solution)/shard_map/ppermute | solution.py:22
  423.3 28.5 %collective-permute-start.14 = (bf16[512,2048]{1,0:T(8,128)(2,1)}, bf16[512,2048]{1,0:T(8,128)(2,1)}, u32[]{:S(2)}, u32[]{:S(2)}) collective-permute-start(bf16[512,2048]{1,0:T(8,128)(2,1)} %collective-permute-done.13), channel_id=1, source_target_pairs={{0,2},{2,4},{4,6},{6,8},{8,10},{10,12},{12,14},{14,16},{16,18},{18... | collective-permute-start | bytes 6291464 | tf_op jit(solution)/shard_map/ppermute | solution.py:22
  423.3 479.1 %reduce-scatter.2.cloned.1.call-start = ((), (), s32[]{:S(2)}) async-start(), calls=%async_computation.3 | async-start | bytes 35651584 | tf_op jit(solution)/shard_map/reduce_scatter | solution.py:29
  423.4 84.3 %copy-start.22 = (bf16[512,2048]{1,0:T(8,128)(2,1)S(1)}, bf16[512,2048]{1,0:T(8,128)(2,1)}, u32[]{:S(2)}) copy-start(bf16[512,2048]{1,0:T(8,128)(2,1)} %copy-done.21) | copy-start | bytes 6291460
  423.4 85.8 %copy-start.20 = (bf16[512,2048]{1,0:T(8,128)(2,1)S(1)}, bf16[512,2048]{1,0:T(8,128)(2,1)}, u32[]{:S(2)}) copy-start(bf16[512,2048]{1,0:T(8,128)(2,1)} %copy-done.19) | copy-start | bytes 6291460
  423.4 93.7 %copy-start.18 = (bf16[512,2048]{1,0:T(8,128)(2,1)S(1)}, bf16[512,2048]{1,0:T(8,128)(2,1)}, u32[]{:S(2)}) copy-start(bf16[512,2048]{1,0:T(8,128)(2,1)} %copy-done.17) | copy-start | bytes 6291460
  423.4 95.2 %copy-start.16 = (bf16[512,2048]{1,0:T(8,128)(2,1)S(1)}, bf16[512,2048]{1,0:T(8,128)(2,1)}, u32[]{:S(2)}) copy-start(bf16[512,2048]{1,0:T(8,128)(2,1)} %copy-done.15) | copy-start | bytes 6291460
  423.5 96.7 %copy-start.14 = (bf16[512,2048]{1,0:T(8,128)(2,1)S(1)}, bf16[512,2048]{1,0:T(8,128)(2,1)}, u32[]{:S(2)}) copy-start(bf16[512,2048]{1,0:T(8,128)(2,1)} %copy-done.13) | copy-start | bytes 6291460
  423.5 98.1 %copy-start.12 = (bf16[512,2048]{1,0:T(8,128)(2,1)S(1)}, bf16[512,2048]{1,0:T(8,128)(2,1)}, u32[]{:S(2)}) copy-start(bf16[512,2048]{1,0:T(8,128)(2,1)} %copy-done.11) | copy-start | bytes 6291460
  423.5 99.6 %copy-start.10 = (bf16[512,2048]{1,0:T(8,128)(2,1)S(1)}, bf16[512,2048]{1,0:T(8,128)(2,1)}, u32[]{:S(2)}) copy-start(bf16[512,2048]{1,0:T(8,128)(2,1)} %copy-done.9) | copy-start | bytes 6291460
  423.5 101.1 %copy-start.8 = (bf16[512,2048]{1,0:T(8,128)(2,1)S(1)}, bf16[512,2048]{1,0:T(8,128)(2,1)}, u32[]{:S(2)}) copy-start(bf16[512,2048]{1,0:T(8,128)(2,1)} %copy-done.7) | copy-start | bytes 6291460
  423.5 102.6 %copy-start.6 = (bf16[512,2048]{1,0:T(8,128)(2,1)S(1)}, bf16[512,2048]{1,0:T(8,128)(2,1)}, u32[]{:S(2)}) copy-start(bf16[512,2048]{1,0:T(8,128)(2,1)} %copy-done.5) | copy-start | bytes 6291460
  423.5 104.1 %copy-start.4 = (bf16[512,2048]{1,0:T(8,128)(2,1)S(1)}, bf16[512,2048]{1,0:T(8,128)(2,1)}, u32[]{:S(2)}) copy-start(bf16[512,2048]{1,0:T(8,128)(2,1)} %copy-done.3) | copy-start | bytes 6291460
  423.5 105.6 %copy-start.2 = (bf16[512,2048]{1,0:T(8,128)(2,1)S(1)}, bf16[512,2048]{1,0:T(8,128)(2,1)}, u32[]{:S(2)}) copy-start(bf16[512,2048]{1,0:T(8,128)(2,1)} %copy-done.1) | copy-start | bytes 6291460
  556.4 346.1 %copy-start.23 = (bf16[256,2048]{1,0:T(8,128)(2,1)S(1)}, bf16[256,2048]{1,0:T(8,128)(2,1)}, u32[]{:S(2)}) copy-start(bf16[256,2048]{1,0:T(8,128)(2,1)} %param.6) | copy-start | bytes 3145732
Sparse Core Ops, SparseCore 0:
  307.6 105.6 all-gather.2
  423.5 58.3 all-gather.4
  574.1 328.3 reduce-scatter.1
